TPU v7x, 128 devices: a whole 4x4x4 slice. The times are simulated.
128 devices in a mesh: dp: 16 (over x, z), table: 8 (over y, core).
Axes of the slice: x: 4, y: 4, z: 4, core: 2. Of those that a mesh axis runs over, the one named last changes fastest.
Arguments:
- touched_rows: bfloat16 [32768, 512], P(('dp', 'table')), may hold values from -6 to 6
- row_of_token: int32 [131072], P(('dp', 'table')), may hold values from 0 to 255
- row_owner: int32 [32768, 1], P(('dp', 'table')), may hold values from 0 to 127; in each aligned block of 256 rows (0 to 255, 256 to 511, ...) at most 4 rows name the same one
- owner_row: int32 [32768], P(('dp', 'table')), may hold values from 0 to 1023
- seq_blocks: int32 [2048], P(('dp', 'table')), may hold values from 1 to 4, as said below
- seq_dest: int32 [2048], P(('dp', 'table')), may hold values from 0 to 15, as said below
- grad_out: bfloat16 [65536, 512], P(('dp', 'table')), may hold values from -6 to 6
- w_in: bfloat16 [512, 2048], replicated, may hold values from -0.25 to 0.25
- w_out: bfloat16 [512, 512], replicated, may hold values from -0.25 to 0.25
- gain_in: float32 [512], replicated, may hold values from 0.25 to 1.75
- gain_out: float32 [512], replicated, may hold values from 0.25 to 1.75
Outputs:
- table_grad: float32 [131072, 512], P(('dp', 'table'))
- grad_w_in: float32 [512, 2048], replicated
- grad_w_out: float32 [512, 512], replicated
- grad_gain_in: float32 [512], replicated
- grad_gain_out: float32 [512], replicated
Inputs may be any that keep to these rules, and one draw needn't show every extreme that they name: `seq_blocks`: lengths in blocks of 16 tokens. The sequences that one device receives total exactly 32 blocks, and among them one has exactly 4 blocks. `seq_dest`: the 16 slots of a device go to 16 different dp indices, so every device receives exactly one sequence from each device with its table index. `row_owner`: at most 4 of one device's touched rows have the same owner.
All inputs are finite; a program needn't handle non-finite values.
Results may differ from a plain program's by a relative error of at most 0.0091.
Values may be sent and summed in bfloat16 or wider, within the bound.
A program may use at most 128 MiB of HBM per device.

v0:
```python
import math

import jax
import jax.numpy as jnp
from jax import lax
from jax.experimental import pallas as pl
from jax.experimental.pallas import tpu as pltpu
from jax.sharding import PartitionSpec as P

HEADS = 4
HDIM = 128
BLK = 16
LMAXB = 4
SLOT = 64
ROWS_DEV = 1024
UNIQ = 256
CAP = 4
D = 512
N_DP = 16
N_TABLE = 8
N_DEV = 128
GROUP = 256
N_GROUP = 4
TOK = 1024
PAIR = 128
CH1 = 48
CH2 = 64
ROWS1 = 96 * CH1
ROWS2 = 96 * CH2
EPSILON = 1e-05
MESH = pl.DeviceIdType.MESH
BF = jnp.bfloat16
F32 = jnp.float32


def dot(a, b):
    return jnp.dot(a, b, preferred_element_type=F32)


def dot_t(a, b):
    return lax.dot_general(a, b, (((1,), (1,)), ((), ())), preferred_element_type=F32)


def t_dot(a, b):
    return lax.dot_general(a, b, (((0,), (0,)), ((), ())), preferred_element_type=F32)


OFFSETS = (
    (0, 1), (1, 0), (3, 0), (0, 3),
    (1, 1), (3, 3), (0, 2), (2, 0),
    (1, 3), (3, 1), (1, 2), (2, 1),
    (3, 2), (2, 3), (2, 2), (0, 0),
)
OWN = 15
ORDERS = (("x", "y", "z"), ("y", "z", "x"), ("z", "x", "y"))


def row_mean(v):
    return jnp.sum(v, axis=-1, keepdims=True) * (1.0 / D)


def sigmoid(v):
    return 0.5 * jnp.tanh(0.5 * v) + 0.5


def iota(shape, dim):
    return lax.broadcasted_iota(jnp.int32, shape, dim)


def step_kernel(
    dest_s,
    dest_l,
    blocks_l,
    items_ref,
    owner_ref,
    orow_ref,
    gin_ref,
    gout_ref,
    touched_hbm,
    grad_hbm,
    w_in_hbm,
    w_out_hbm,
    g1_ref,
    g2_ref,
    got_ref,
    gotm_ref,
    gains_ref,
    touched,
    grad_bal,
    w_in,
    w_out,
    load_sem,
    lens,
    got_len,
    wide,
    stage,
    ret,
    lsem,
    dsem,
    own_sem,
    hot_all,
    norm_t,
    mixed_t,
    hat_in_all,
    rstd_in_all,
    hat_out_all,
    rstd_out_all,
    slope_all,
    gate_all,
    vqk_all,
    att,
    wts,
    half_all,
    gh_all,
    rows_acc,
    gains_acc,
    spread,
    send,
    meta,
    a1,
    a2,
    pr1,
    pr2,
    b1,
    b2,
    fr1,
    fr2,
    c1,
    c2,
    sr1,
    sr2,
    tr1,
    tr2,
    gbuf,
    psem,
    rsem,
    asem,
    gsem,
):
    dp = lax.axis_index("dp")
    tb = lax.axis_index("table")
    x = dp // 4
    z = dp % 4
    y = tb // 2
    core = tb % 2
    me = dp * N_TABLE + tb
    partner = (dp, y * 2 + 1 - core)
    coords = {"x": x, "y": y, "z": z}

    def device(i):
        other = lax.rem(me + i, N_DEV)
        return other, (other // N_TABLE, other % N_TABLE)

    def along(axis, d):
        v = lax.rem(coords[axis] + d, 4)
        to = {"x": (v * 4 + z, tb), "z": (x * 4 + v, tb), "y": (dp, v * 2 + core)}[axis]
        return v, to

    def plus(i):
        dx, dz = OFFSETS[i]
        return lax.rem(x + dx, 4) * 4 + lax.rem(z + dz, 4)

    def minus(i):
        dx, dz = OFFSETS[i]
        return lax.rem(x + 4 - dx, 4) * 4 + lax.rem(z + 4 - dz, 4)

    def remote(src, dst, sems, index, to):
        return pltpu.make_async_remote_copy(
            src_ref=src,
            dst_ref=dst,
            send_sem=sems.at[(0,) + index],
            recv_sem=sems.at[(1,) + index],
            device_id=to,
            device_id_type=MESH,
        )

    loads = [
        pltpu.make_async_copy(touched_hbm, touched, load_sem.at[0]),
        pltpu.make_async_copy(w_in_hbm, w_in, load_sem.at[1]),
        pltpu.make_async_copy(grad_hbm, grad_bal, load_sem.at[2]),
        pltpu.make_async_copy(w_out_hbm, w_out, load_sem.at[3]),
    ]
    for load in loads:
        load.start()

    barrier = pltpu.get_barrier_semaphore()

    def greet(i, carry):
        pl.semaphore_signal(barrier, inc=1, device_id=device(i)[1], device_id_type=MESH)
        return carry

    lax.fori_loop(1, N_DEV, greet, 0)

    hits = dest_l[...] == iota((N_DP, N_DP), 0)
    lengths = jnp.sum(
        jnp.where(hits, blocks_l[...].astype(F32), 0.0), axis=1, keepdims=True
    )
    lengths = jnp.broadcast_to(lengths, (N_DP, D)).astype(jnp.int32)
    for p in range(N_DP):
        lens[p] = lengths[p : p + 1, :]

    gain_in = gin_ref[...]
    gain_out = gout_ref[...]
    gains_acc[...] = jnp.zeros_like(gains_acc)
    lane = iota((1, 128), 1)

    def item_pair(i):
        rows = []
        for k in range(2):
            peer = plus(i + k)
            slot = jnp.int32(0)
            for j in range(N_DP):
                slot = jnp.where(dest_s[j] == peer, j, slot)
            row = items_ref[pl.ds(slot // 2, 1), :]
            turned = pltpu.roll(row, 64, 1)
            rows.append(jnp.where(jnp.broadcast_to(slot % 2, (1, 128)) == k, row, turned))
        return jnp.where(lane < 64, rows[0], rows[1])

    def forward(g):
        here = slice(g * GROUP, (g + 1) * GROUP)
        items = jnp.concatenate([item_pair(4 * g), item_pair(4 * g + 2)], axis=1)
        hot = (iota((UNIQ, GROUP), 0) == items).astype(F32).astype(BF)
        hot_all[:, here] = hot
        tok = t_dot(hot, touched[...])
        shifted = tok - row_mean(tok)
        rstd = lax.rsqrt(row_mean(shifted * shifted) + EPSILON)
        rstd_in_all[here, :] = rstd
        hat = shifted * rstd
        hat_in_all[here, :] = hat
        normed = hat * gain_in
        norm_t[:, here] = jnp.transpose(normed).astype(BF)
        normed = normed.astype(BF)
        for k in range(4):
            cols = slice(k * D, (k + 1) * D)
            hid = dot(normed, w_in[:, cols])
            sig = sigmoid(hid)
            act = hid * sig
            slope_all[here, cols] = sig + act * (1.0 - sig)
            if k == 0:
                gate_all[here, :] = act
            else:
                vqk_all[k - 1, here, :] = act.astype(BF)
        ri = iota((PAIR, PAIR), 0)
        ci = iota((PAIR, PAIR), 1)
        allowed = ((ri < SLOT) == (ci < SLOT)) & (ci <= ri)
        scale = HDIM ** (-0.5)
        for s in range(2):
            rows = slice(g * GROUP + s * PAIR, g * GROUP + (s + 1) * PAIR)
            for h in range(HEADS):
                cols = slice(h * HDIM, (h + 1) * HDIM)
                n = (g * 2 + s) * HEADS + h
                score = dot_t(vqk_all[1, rows, cols], vqk_all[2, rows, cols]) * scale
                sig = sigmoid(score)
                act = score * sig
                weight = jnp.where(allowed, act, 0.0).astype(BF)
                wts[n, 0] = weight
                wts[n, 1] = jnp.where(allowed, (sig + act * (1.0 - sig)) * scale, 0.0).astype(BF)
                att[s * PAIR : (s + 1) * PAIR, cols] = dot(weight, vqk_all[0, rows, cols])
        attended = att[...]
        shifted = attended - row_mean(attended)
        rstd = lax.rsqrt(row_mean(shifted * shifted) + EPSILON)
        rstd_out_all[here, :] = rstd
        hat = shifted * rstd
        hat_out_all[here, :] = hat
        mixed_t[:, here] = jnp.transpose(hat * gain_out * gate_all[here, :]).astype(BF)

    loads[0].wait()
    loads[1].wait()
    forward(0)

    pl.semaphore_wait(barrier, N_DEV - 1)

    def len_copy(i):
        return remote(lens.at[minus(i)], got_len.at[dp], lsem, (i,), (minus(i), tb))

    for i in range(OWN):
        len_copy(i).start()
    got_len[dp] = lens[dp]
    forward(1)
    for i in range(OWN):
        len_copy(i).wait()
    loads[2].wait()
    loads[3].wait()

    start = jnp.zeros((1, D), jnp.int32)
    for p in range(N_DP):
        wide[p] = start
        start = start + got_len[p]
    row_id = iota((SLOT, D), 0)
    col_id = iota((SLOT, D), 1)

    def staged(p):
        hit = (col_id == wide[p] * BLK + row_id) & (row_id < got_len[p] * BLK)
        return dot(hit.astype(F32).astype(BF), grad_bal[...]).astype(BF)

    def data_copy(i):
        return remote(stage.at[i], ret.at[i], dsem, (i,), (minus(i), tb))

    for i in range(OWN):
        stage[i] = staged(minus(i))
        data_copy(i).start()
    ret[OWN] = staged(dp)

    forward(2)
    forward(3)

    def back_a(g):
        here = slice(g * GROUP, (g + 1) * GROUP)
        gy = ret[4 * g : 4 * g + 4].reshape(GROUP, D)
        hat = hat_out_all[here, :]
        grad_mixed = dot_t(gy, w_out[...])
        gh_all[here, 0:D] = (grad_mixed * (hat * gain_out) * slope_all[here, 0:D]).astype(BF)
        cot = grad_mixed * gate_all[here, :]
        gains_acc[1:2, :] += jnp.sum(cot * hat, axis=0, keepdims=True)
        dhat = cot * gain_out
        half_all[here, :] = (
            rstd_out_all[here, :] * (dhat - row_mean(dhat) - hat * row_mean(dhat * hat))
        ).astype(BF)

    def back_b(g):
        for s in range(2):
            rows = slice(g * GROUP + s * PAIR, g * GROUP + (s + 1) * PAIR)
            for h in range(HEADS):
                cols = slice(h * HDIM, (h + 1) * HDIM)
                n = (g * 2 + s) * HEADS + h
                half = half_all[rows, cols]
                grad_weight = dot_t(half, vqk_all[0, rows, cols])
                gs = (grad_weight * wts[n, 1].astype(F32)).astype(BF)
                parts = (
                    t_dot(wts[n, 0], half),
                    dot(gs, vqk_all[2, rows, cols]),
                    t_dot(gs, vqk_all[1, rows, cols]),
                )
                for k in range(3):
                    at = slice((k + 1) * D + h * HDIM, (k + 1) * D + (h + 1) * HDIM)
                    gh_all[rows, at] = (parts[k] * slope_all[rows, at]).astype(BF)

    def back_c(g):
        here = slice(g * GROUP, (g + 1) * GROUP)
        gy = ret[4 * g : 4 * g + 4].reshape(GROUP, D).astype(F32)
        hat = hat_in_all[here, :]
        grad_normed = dot_t(gh_all[here, :], w_in[...])
        gains_acc[0:1, :] += jnp.sum(grad_normed * hat, axis=0, keepdims=True)
        dhat = grad_normed * gain_in
        inner = rstd_in_all[here, :] * (dhat - row_mean(dhat) - hat * row_mean(dhat * hat))
        grad_tok = (inner + gy).astype(BF)
        part = dot(hot_all[:, here], grad_tok)
        if g == 0:
            rows_acc[...] = part
        else:
            rows_acc[...] += part

    def put(dst, first, block):
        for j in range(4):
            dst[first + j * D : first + (j + 1) * D, :] = block[:, j * 128 : (j + 1) * 128].astype(BF)

    def all_reduce(s, ch, a, pr, b, fr, c, sr, tr, out):
        third = 16 * ch
        quarter = 4 * ch

        def at(row, size):
            return pl.ds(pl.multiple_of(row, 16), size)

        def pair(q):
            src = a.at[at(((1 - core) * 3 + q) * third, third)]
            return remote(src, pr.at[q], psem, (s, 0, q), partner)

        def first(q, d):
            v, to = along(ORDERS[q][0], d)
            return remote(b.at[q, at(v * quarter, quarter)], fr.at[q, d - 1], rsem, (s, 0, q, d - 1), to)

        def second(q, d):
            v, to = along(ORDERS[q][1], d)
            return remote(c.at[q, at(v * ch, ch)], sr.at[q, d - 1], rsem, (s, 1, q, d - 1), to)

        def third_copy(q, d):
            mine = coords[ORDERS[q][2]]
            to = along(ORDERS[q][2], d)[1]
            return remote(tr.at[q, mine], tr.at[q, mine], rsem, (s, 2, q, d - 1), to)

        def row_of(q, depth):
            row = (core * 3 + q) * third
            if depth > 0:
                row = row + coords[ORDERS[q][0]] * quarter
            if depth > 1:
                row = row + coords[ORDERS[q][1]] * ch
            return row

        def back_two(q, d):
            ref = out.at[at(row_of(q, 2), ch)]
            return remote(ref, ref, rsem, (s, 3, q, d - 1), along(ORDERS[q][1], d)[1])

        def back_one(q, d):
            ref = out.at[at(row_of(q, 1), quarter)]
            return remote(ref, ref, rsem, (s, 4, q, d - 1), along(ORDERS[q][0], d)[1])

        def back_pair(q):
            ref = out.at[at(row_of(q, 0), third)]
            return remote(ref, ref, psem, (s, 1, q), partner)

        for q in range(3):
            pair(q).start()
        yield
        for q in range(3):
            pair(q).wait()

            def add0(k, carry, q=q):
                rows = at(k * quarter, quarter)
                own = a[at((core * 3 + q) * third + k * quarter, quarter), :].astype(F32)
                b[q, rows, :] = (own + pr[q, rows, :].astype(F32)).astype(BF)
                return carry

            lax.fori_loop(0, 4, add0, 0)
            for d in range(1, 4):
                first(q, d).start()
        yield
        for q in range(3):
            for d in range(1, 4):
                first(q, d).wait()
            total = b[q, at(coords[ORDERS[q][0]] * quarter, quarter), :].astype(F32)
            for d in range(3):
                total = total + fr[q, d].astype(F32)
            c[q] = total.astype(BF)
            for d in range(1, 4):
                second(q, d).start()
        yield
        for q in range(3):
            for d in range(1, 4):
                second(q, d).wait()
            total = c[q, at(coords[ORDERS[q][1]] * ch, ch), :].astype(F32)
            for d in range(3):
                total = total + sr[q, d].astype(F32)
            tr[q, coords[ORDERS[q][2]]] = total.astype(BF)
            for d in range(1, 4):
                third_copy(q, d).start()
        yield
        for q in range(3):
            for d in range(1, 4):
                third_copy(q, d).wait()
            total = tr[q, 0].astype(F32)
            for d in range(1, 4):
                total = total + tr[q, d].astype(F32)
            out[at(row_of(q, 2), ch), :] = total.astype(BF)
            for d in range(1, 4):
                back_two(q, d).start()
        yield
        for q in range(3):
            for d in range(1, 4):
                back_two(q, d).wait()
            for d in range(1, 4):
                back_one(q, d).start()
        yield
        for q in range(3):
            for d in range(1, 4):
                back_one(q, d).wait()
            back_pair(q).start()
        yield
        for q in range(3):
            back_pair(q).wait()
        yield

    def gain_reduce():
        def pair():
            ref = gbuf.at[0, core]
            return remote(ref, ref, gsem, (0, 0), partner)

        def copy(k, d):
            axis = "xyz"[k - 1]
            ref = gbuf.at[k, coords[axis]]
            return remote(ref, ref, gsem, (k, d - 1), along(axis, d)[1])

        gbuf[0, core] = jnp.concatenate(
            [gains_acc[r : r + 1, j * 128 : (j + 1) * 128] for r in range(2) for j in range(4)],
            axis=0,
        )
        pair().start()
        yield
        pair().wait()
        total = gbuf[0, 0] + gbuf[0, 1]
        for k in range(1, 4):
            gbuf[k, coords["xyz"[k - 1]]] = total
            for d in range(1, 4):
                copy(k, d).start()
            yield
            for d in range(1, 4):
                copy(k, d).wait()
            total = (gbuf[k, 0] + gbuf[k, 1]) + (gbuf[k, 2] + gbuf[k, 3])
        gains_ref[...] = total
        yield

    red1 = all_reduce(0, CH1, a1, pr1, b1, fr1, c1, sr1, tr1, g1_ref)
    red2 = all_reduce(1, CH2, a2, pr2, b2, fr2, c2, sr2, tr2, g2_ref)
    red_g = gain_reduce()

    for g in range(N_GROUP):
        for i in range(4 * g, min(4 * g + 4, OWN)):
            data_copy(i).wait_recv()
        back_a(g)
    put(a1, 0, dot(mixed_t[...], ret[...].reshape(TOK, D)))
    put(a1, 4 * D, dot(norm_t[...], gh_all[:, 0:D]))
    a1[8 * D : ROWS1, :] = jnp.zeros((ROWS1 - 8 * D, 128), BF)
    next(red1)
    back_b(0)
    next(red1)
    back_b(1)
    back_b(2)
    next(red1)
    back_b(3)
    for k in range(3):
        put(a2, k * 4 * D, dot(norm_t[...], gh_all[:, (k + 1) * D : (k + 2) * D]))
    next(red2)
    next(red1)
    back_c(0)
    next(red2)
    next(red1)
    back_c(1)
    next(red1)
    back_c(2)
    next(red2)
    back_c(3)

    owner = jnp.broadcast_to(owner_ref[...].astype(F32), (UNIQ, UNIQ))
    owner_col = jnp.transpose(owner)
    before = iota((UNIQ, UNIQ), 0) < iota((UNIQ, UNIQ), 1)
    rank = jnp.sum(jnp.where((owner == owner_col) & before, 1.0, 0.0), axis=0, keepdims=True)
    mine = iota((N_DEV, UNIQ), 0) == owner_ref[...]
    lanes = iota((N_DEV, 128), 1)
    row_half = rows_acc[...].astype(BF)
    ids_all = jnp.zeros((N_DEV, 128), F32)
    order_f = orow_ref[...].astype(F32)
    for c in range(CAP):
        sel = jnp.where(mine & (rank == float(c)), 1.0, 0.0)
        ids = jnp.sum(sel * order_f, axis=1, keepdims=True)
        ids_all = jnp.where(lanes == c, ids, ids_all)
        picked = dot(sel.astype(BF), row_half)
        for k in range(4):
            spread[pl.ds(k * CAP + c, N_DEV, stride=16), :] = picked[:, k * 128 : (k + 1) * 128]
    send[...] = spread[...].astype(BF).reshape(N_DEV, 16, 128)
    meta[...] = ids_all.reshape(N_DEV, 1, 128)

    next(red_g)

    def scatter_out(i, carry):
        other, to = device(i)
        remote(send.at[other], got_ref.at[i], asem, (0,), to).start()
        remote(meta.at[other], gotm_ref.at[i], asem, (1,), to).start()
        return carry

    lax.fori_loop(1, N_DEV, scatter_out, 0)
    got_ref[0] = send[me]
    gotm_ref[0] = meta[me]

    next(red2)
    next(red_g)
    next(red1)
    next(red2)
    next(red_g)
    next(red2)
    next(red_g)
    next(red2)
    next(red_g)
    next(red1)
    others = pl.ds(1, N_DEV - 1)
    remote(send.at[others], got_ref.at[others], asem, (0,), partner).wait()
    remote(meta.at[others], gotm_ref.at[others], asem, (1,), partner).wait()
    for i in range(OWN):
        data_copy(i).wait_send()
    next(red2)


def run_step(seq_dest, seq_blocks, items, owner, orow, gain_in, gain_out, touched, grad_out, w_in, w_out):
    smem = pl.BlockSpec(memory_space=pltpu.SMEM)
    vmem = pl.BlockSpec(memory_space=pltpu.VMEM)
    far = pl.BlockSpec(memory_space=pl.ANY)
    v = pltpu.VMEM
    dma = pltpu.SemaphoreType.DMA
    scratch = [
        v((UNIQ, D), BF),
        v((D, D), BF),
        v((D, 4 * D), BF),
        v((D, D), BF),
        dma((4,)),
        v((N_DP, 1, D), jnp.int32),
        v((N_DP, 1, D), jnp.int32),
        v((N_DP, 1, D), jnp.int32),
        v((N_DP, SLOT, D), BF),
        v((N_DP, SLOT, D), BF),
        dma((2, N_DP)),
        dma((2, N_DP)),
        dma((1,)),
        v((UNIQ, TOK), BF),
        v((D, TOK), BF),
        v((D, TOK), BF),
        v((TOK, D), F32),
        v((TOK, 1), F32),
        v((TOK, D), F32),
        v((TOK, 1), F32),
        v((TOK, 4 * D), F32),
        v((TOK, D), F32),
        v((3, TOK, D), BF),
        v((GROUP, D), F32),
        v((N_GROUP * 2 * HEADS, 2, PAIR, PAIR), BF),
        v((TOK, D), BF),
        v((TOK, 4 * D), BF),
        v((UNIQ, D), F32),
        v((8, D), F32),
        v((N_DEV * 16, 128), F32),
        v((N_DEV, 16, 128), BF),
        v((N_DEV, 1, 128), F32),
        v((ROWS1, 128), BF),
        v((ROWS2, 128), BF),
    ]
    for shape in ((3, 16), (3, 16), (3, 3, 4), (3, 4), (3, 3, 1), (3, 4, 1)):
        for ch in (CH1, CH2):
            scratch.append(v(shape[:-1] + (shape[-1] * ch, 128), BF))
    scratch += [
        v((4, 4, 8, 128), F32),
        dma((2, 2, 2, 3)),
        dma((2, 2, 5, 3, 3)),
        dma((2, 2)),
        dma((2, 4, 3)),
    ]
    return pl.pallas_call(
        step_kernel,
        out_shape=(
            jax.ShapeDtypeStruct((ROWS1, 128), BF),
            jax.ShapeDtypeStruct((ROWS2, 128), BF),
            jax.ShapeDtypeStruct((N_DEV, 16, 128), BF),
            jax.ShapeDtypeStruct((N_DEV, 1, 128), F32),
            jax.ShapeDtypeStruct((8, 128), F32),
        ),
        in_specs=[smem] + [vmem] * 7 + [far] * 4,
        out_specs=(vmem,) * 5,
        scratch_shapes=scratch,
        compiler_params=pltpu.CompilerParams(
            collective_id=0, has_side_effects=True, vmem_limit_bytes=67_000_000
        ),
        name="step",
    )(
        seq_dest,
        seq_dest.reshape(1, -1),
        seq_blocks.reshape(1, -1),
        items.reshape(8, 128),
        owner.reshape(1, -1),
        orow.reshape(1, -1),
        gain_in.reshape(1, -1),
        gain_out.reshape(1, -1),
        touched,
        grad_out,
        w_in,
        w_out,
    )


def finish_kernel(
    out_ref, gate_ref, rest_ref, got_ref, meta_ref, gains_in, table_ref, win_ref, wout_ref, gin_ref, gout_ref, spread, picked, ids, *, factor
):
    i = pl.program_id(0)

    def unpack(src, dst):
        for j in range(4):
            dst[:, j * 128 : (j + 1) * 128] = src[j * D : (j + 1) * D, :].astype(F32) * factor

    @pl.when(i == 0)
    def _():
        spread[...] = got_ref[...].astype(F32)
        for c in range(CAP):
            for k in range(4):
                picked[c * N_DEV : (c + 1) * N_DEV, k * 128 : (k + 1) * 128] = spread[
                    pl.ds(k * CAP + c, N_DEV, stride=16), :
                ].astype(BF)
        ids[...] = jnp.transpose(meta_ref[...].reshape(N_DEV, 128))
        for j in range(4):
            gin_ref[:, j * 128 : (j + 1) * 128] = gains_in[j : j + 1, :] * factor
            gout_ref[:, j * 128 : (j + 1) * 128] = gains_in[4 + j : 5 + j, :] * factor
        unpack(out_ref, wout_ref)
        unpack(gate_ref, win_ref)

    @pl.when(i > 0)
    def _():
        unpack(rest_ref, win_ref)

    rows = (iota((256, N_DEV), 0) + i * 256).astype(F32)
    hot = jnp.concatenate(
        [jnp.where(rows == ids[c : c + 1, :], 1.0, 0.0).astype(BF) for c in range(CAP)], axis=1
    )
    table_ref[...] = dot(hot, picked[...])


def finish(g1, g2, got, meta, gains, factor):
    def fixed(*shape):
        return pl.BlockSpec(shape, lambda i: (0,) * len(shape))

    def body(*refs):
        finish_kernel(*refs, factor=factor)

    return pl.pallas_call(
        body,
        out_shape=(
            jax.ShapeDtypeStruct((ROWS_DEV, D), F32),
            jax.ShapeDtypeStruct((D, 4 * D), F32),
            jax.ShapeDtypeStruct((D, D), F32),
            jax.ShapeDtypeStruct((1, D), F32),
            jax.ShapeDtypeStruct((1, D), F32),
        ),
        grid=(4,),
        in_specs=[
            pl.BlockSpec((4 * D, 128), lambda i: (0, 0)),
            pl.BlockSpec((4 * D, 128), lambda i: (1, 0)),
            pl.BlockSpec((4 * D, 128), lambda i: (jnp.maximum(i - 1, 0), 0)),
            fixed(N_DEV * 16, 128),
            fixed(N_DEV, 1, 128),
            fixed(8, 128),
        ],
        out_specs=(
            pl.BlockSpec((256, D), lambda i: (i, 0)),
            pl.BlockSpec((D, D), lambda i: (0, i)),
            fixed(D, D),
            fixed(1, D),
            fixed(1, D),
        ),
        scratch_shapes=[
            pltpu.VMEM((N_DEV * 16, 128), F32),
            pltpu.VMEM((CAP * N_DEV, D), BF),
            pltpu.VMEM((128, N_DEV), F32),
        ],
        compiler_params=pltpu.CompilerParams(vmem_limit_bytes=40 << 20),
        name="finish",
    )(g1, g1, g2, got.reshape(N_DEV * 16, 128), meta, gains)


def on_device(
    touched_rows,
    row_of_token,
    row_owner,
    owner_row,
    seq_blocks,
    seq_dest,
    grad_out,
    w_in,
    w_out,
    gain_in,
    gain_out,
):
    g1, g2, got, meta, gains = run_step(
        seq_dest,
        seq_blocks,
        row_of_token,
        row_owner,
        owner_row,
        gain_in,
        gain_out,
        touched_rows,
        grad_out,
        w_in,
        w_out,
    )
    factor = 1.0 / math.sqrt(grad_out.shape[0] * N_DEV)
    table, grad_in, grad_w_out, gin, gout = finish(g1, g2, got, meta, gains, factor)
    return (table, grad_in, grad_w_out, gin.reshape(-1), gout.reshape(-1))


def solution(mesh):
    in_specs = (
        P(("dp", "table"), None),
        P(("dp", "table")),
        P(("dp", "table"), None),
        P(("dp", "table")),
        P(("dp", "table")),
        P(("dp", "table")),
        P(("dp", "table"), None),
        P(),
        P(),
        P(),
        P(),
    )
    out_specs = (P(("dp", "table"), None), P(), P(), P(), P())
    return jax.shard_map(
        on_device, mesh=mesh, in_specs=in_specs, out_specs=out_specs, check_vma=False
    )
```

profile of v0, /device:TPU:1, one launch (start us, length us, event | category | flops | bytes accessed | tf_op | source)
XLA Modules:
  0.0 90.9 jit_solution(10499191367406026154)
XLA Ops:
  0.6 81.0 %step.1 = (bf16[4608,128]{1,0:T(8,128)(2,1)}, bf16[6144,128]{1,0:T(8,128)(2,1)}, bf16[128,16,128]{2,1,0:T(8,128)(2,1)}, f32[128,1,128]{2,1,0:T(1,128)}, f32[8,128]{1,0:T(8,128)}) custom-call(s32[16]{0:T(128)} %dest_s.1, s32[1,16]{1,0:T(1,128)} %bitcast.14, s32[1,16]{1,0:T(1,128)} %bitcast.17, s32[8,128]{1,0:T(8,128)} %bitcast.11, s32[1,256]{1,0:T(1,128)} %bitcast.15, ...), custom_call_target="tpu_custom_call" | custom-call | tf_op jit(solution)/shard_map/step/pallas_call | solution.py:623
  81.6 0.0 copy-start
  81.6 1.3 %copy-done = bf16[4608,128]{1,0:T(8,128)(2,1)S(1)} copy-done((bf16[4608,128]{1,0:T(8,128)(2,1)S(1)}, bf16[4608,128]{1,0:T(8,128)(2,1)}, u32[]{:S(2)}) %copy-start) | copy-done | bytes 1179672
  82.9 0.0 copy-start.1
  82.9 1.4 %copy-done.1 = bf16[6144,128]{1,0:T(8,128)(2,1)S(1)} copy-done((bf16[6144,128]{1,0:T(8,128)(2,1)S(1)}, bf16[6144,128]{1,0:T(8,128)(2,1)}, u32[]{:S(2)}) %copy-start.1) | copy-done | bytes 1572888
  84.3 0.0 copy-start.2
  84.3 1.0 %copy-done.2 = bf16[128,16,128]{2,1,0:T(8,128)(2,1)S(1)} copy-done((bf16[128,16,128]{2,1,0:T(8,128)(2,1)S(1)}, bf16[128,16,128]{2,1,0:T(8,128)(2,1)}, u32[]{:S(2)}) %copy-start.2) | copy-done | bytes 524312
  85.4 0.0 copy-start.3
  85.4 0.8 copy-done.3
  86.2 0.0 copy-start.4
  86.2 0.7 copy-done.4
  86.9 4.0 %finish.1 = (f32[1024,512]{1,0:T(8,128)}, f32[512,2048]{1,0:T(8,128)}, f32[512,512]{1,0:T(8,128)}, f32[1,512]{1,0:T(1,128)}, f32[1,512]{1,0:T(1,128)}) custom-call(bf16[4608,128]{1,0:T(8,128)(2,1)S(1)} %copy-done, bf16[4608,128]{1,0:T(8,128)(2,1)S(1)} %copy-done, bf16[6144,128]{1,0:T(8,128)(2,1)S(1)} %copy-done.1, bf16[2048,128]{1,0:T(8,128)(2,1)S(1)} %bitcast.10, ...), custom_call_target="tpu_custom_call" | custom-call | tf_op jit(solution)/shard_map/finish/pallas_call | solution.py:697
Async XLA Ops:
  81.6 1.3 %copy-start = (bf16[4608,128]{1,0:T(8,128)(2,1)S(1)}, bf16[4608,128]{1,0:T(8,128)(2,1)}, u32[]{:S(2)}) copy-start(bf16[4608,128]{1,0:T(8,128)(2,1)} %get-tuple-element.15.refs_0_.refs_1_) | copy-start | bytes 3538948
  82.9 1.4 %copy-start.1 = (bf16[6144,128]{1,0:T(8,128)(2,1)S(1)}, bf16[6144,128]{1,0:T(8,128)(2,1)}, u32[]{:S(2)}) copy-start(bf16[6144,128]{1,0:T(8,128)(2,1)} %get-tuple-element.16.refs_2_) | copy-start | bytes 4718596
  84.3 1.0 %copy-start.2 = (bf16[128,16,128]{2,1,0:T(8,128)(2,1)S(1)}, bf16[128,16,128]{2,1,0:T(8,128)(2,1)}, u32[]{:S(2)}) copy-start(bf16[128,16,128]{2,1,0:T(8,128)(2,1)} %get-tuple-element.17) | copy-start | bytes 1572868
  85.4 0.8 copy-start.3
  86.2 0.7 copy-start.4
where the time goes:
time: 91.2 us; the launch traced here: 90.9 us
  Pallas kernels  85 us (93%)
  local copies, waits for them, and re-layouts  5.23 us (6%)
    pallas_call x1, Pallas kernels, run_step(): pl.pallas_call(step_kernel, out_shape=(jax.ShapeDtypeStruct((ROWS1, 128),...  81 us
    unnamed x10, local copies, waits for them, and re-layouts  5.23 us
    pallas_call x1, Pallas kernels, finish(): pl.pallas_call(body, out_shape=(jax.ShapeDtypeStruct((ROWS_DEV, D), F32),...  3.97 us

commit v1 on v0

--- a/solution.py
+++ b/solution.py
@@ -117,6 +117,7 @@
     spread,
     send,
     meta,
+    sel_all,
     a1,
     a2,
     pr1,
@@ -134,6 +135,7 @@
     gbuf,
     psem,
     rsem,
+    bsem,
     asem,
     gsem,
 ):
@@ -276,6 +278,19 @@
     for i in range(OWN):
         len_copy(i).start()
     got_len[dp] = lens[dp]
+    owner = jnp.broadcast_to(owner_ref[...].astype(F32), (UNIQ, UNIQ))
+    owner_col = jnp.transpose(owner)
+    before = iota((UNIQ, UNIQ), 0) < iota((UNIQ, UNIQ), 1)
+    rank = jnp.sum(jnp.where((owner == owner_col) & before, 1.0, 0.0), axis=0, keepdims=True)
+    mine = iota((N_DEV, UNIQ), 0) == owner_ref[...]
+    lanes = iota((N_DEV, 128), 1)
+    ids_all = jnp.zeros((N_DEV, 128), F32)
+    order_f = orow_ref[...].astype(F32)
+    for c in range(CAP):
+        sel = jnp.where(mine & (rank == float(c)), 1.0, 0.0)
+        sel_all[c] = sel.astype(BF)
+        ids_all = jnp.where(lanes == c, jnp.sum(sel * order_f, axis=1, keepdims=True), ids_all)
+    meta[...] = ids_all.reshape(N_DEV, 1, 128)
     forward(1)
     for i in range(OWN):
         len_copy(i).wait()
@@ -289,17 +304,32 @@
     row_id = iota((SLOT, D), 0)
     col_id = iota((SLOT, D), 1)
 
-    def staged(p):
+    def pick(p):
         hit = (col_id == wide[p] * BLK + row_id) & (row_id < got_len[p] * BLK)
-        return dot(hit.astype(F32).astype(BF), grad_bal[...]).astype(BF)
+        return hit.astype(F32).astype(BF)
 
     def data_copy(i):
         return remote(stage.at[i], ret.at[i], dsem, (i,), (minus(i), tb))
 
-    for i in range(OWN):
-        stage[i] = staged(minus(i))
-        data_copy(i).start()
-    ret[OWN] = staged(dp)
+    for g in range(N_GROUP):
+        hot = jnp.concatenate([pick(minus(4 * g + k)) for k in range(4)], axis=0)
+        slabs = dot(hot, grad_bal[...]).astype(BF)
+        for k in range(4):
+            i = 4 * g + k
+            slab = slabs[k * SLOT : (k + 1) * SLOT, :]
+            if i == OWN:
+                ret[OWN] = slab
+            else:
+                stage[i] = slab
+                data_copy(i).start()
+
+    def meta_out(i, carry):
+        other, to = device(i)
+        remote(meta.at[other], gotm_ref.at[i], asem, (1,), to).start()
+        return carry
+
+    lax.fori_loop(1, N_DEV, meta_out, 0)
+    gotm_ref[0] = meta[me]
 
     forward(2)
     forward(3)
@@ -361,9 +391,16 @@
         def at(row, size):
             return pl.ds(pl.multiple_of(row, 16), size)
 
-        def pair(q):
-            src = a.at[at(((1 - core) * 3 + q) * third, third)]
-            return remote(src, pr.at[q], psem, (s, 0, q), partner)
+        def pair(q, d):
+            v = along(ORDERS[q][0], d)[0]
+            src = a.at[at(((1 - core) * 3 + q) * third + v * quarter, quarter)]
+            return remote(src, pr.at[q, at(v * quarter, quarter)], psem, (s, 0, q, d), partner)
+
+        def add_pair(q, d):
+            v = along(ORDERS[q][0], d)[0]
+            own = a[at((core * 3 + q) * third + v * quarter, quarter), :].astype(F32)
+            rows = at(v * quarter, quarter)
+            b[q, rows, :] = (own + pr[q, rows, :].astype(F32)).astype(BF)
 
         def first(q, d):
             v, to = along(ORDERS[q][0], d)
@@ -378,41 +415,34 @@
             to = along(ORDERS[q][2], d)[1]
             return remote(tr.at[q, mine], tr.at[q, mine], rsem, (s, 2, q, d - 1), to)
 
-        def row_of(q, depth):
-            row = (core * 3 + q) * third
-            if depth > 0:
-                row = row + coords[ORDERS[q][0]] * quarter
-            if depth > 1:
-                row = row + coords[ORDERS[q][1]] * ch
-            return row
+        def piece(q, da, db):
+            va = along(ORDERS[q][0], 4 - da)[0]
+            vb = along(ORDERS[q][1], 4 - db)[0]
+            return at((core * 3 + q) * third + va * quarter + vb * ch, ch)
 
         def back_two(q, d):
-            ref = out.at[at(row_of(q, 2), ch)]
+            ref = out.at[piece(q, 0, 0)]
             return remote(ref, ref, rsem, (s, 3, q, d - 1), along(ORDERS[q][1], d)[1])
 
-        def back_one(q, d):
-            ref = out.at[at(row_of(q, 1), quarter)]
-            return remote(ref, ref, rsem, (s, 4, q, d - 1), along(ORDERS[q][0], d)[1])
-
-        def back_pair(q):
-            ref = out.at[at(row_of(q, 0), third)]
-            return remote(ref, ref, psem, (s, 1, q), partner)
-
-        for q in range(3):
-            pair(q).start()
-        yield
-        for q in range(3):
-            pair(q).wait()
-
-            def add0(k, carry, q=q):
-                rows = at(k * quarter, quarter)
-                own = a[at((core * 3 + q) * third + k * quarter, quarter), :].astype(F32)
-                b[q, rows, :] = (own + pr[q, rows, :].astype(F32)).astype(BF)
-                return carry
-
-            lax.fori_loop(0, 4, add0, 0)
-            for d in range(1, 4):
-                first(q, d).start()
+        def back_one(q, d, k):
+            ref = out.at[piece(q, 0, k)]
+            return remote(ref, ref, bsem, (s, q, d - 1, k), along(ORDERS[q][0], d)[1])
+
+        def back_pair(q, d):
+            va = along(ORDERS[q][0], 4 - d)[0]
+            ref = out.at[at((core * 3 + q) * third + va * quarter, quarter)]
+            return remote(ref, ref, psem, (s, 1, q, d), partner)
+
+        for d in (2, 1, 3, 0):
+            for q in range(3):
+                pair(q, d).start()
+        yield
+        for d in (2, 1, 3, 0):
+            for q in range(3):
+                pair(q, d).wait()
+                add_pair(q, d)
+                if d:
+                    first(q, d).start()
         yield
         for q in range(3):
             for d in range(1, 4):
@@ -440,23 +470,29 @@
             total = tr[q, 0].astype(F32)
             for d in range(1, 4):
                 total = total + tr[q, d].astype(F32)
-            out[at(row_of(q, 2), ch), :] = total.astype(BF)
-            for d in range(1, 4):
+            out[piece(q, 0, 0), :] = total.astype(BF)
+            for d in (2, 1, 3):
                 back_two(q, d).start()
-        yield
+            for d in (2, 1, 3):
+                back_one(q, d, 0).start()
+        yield
+        for k in (1, 3, 2):
+            for q in range(3):
+                back_two(q, k).wait()
+                for d in (2, 1, 3):
+                    back_one(q, d, k).start()
         for q in range(3):
-            for d in range(1, 4):
-                back_two(q, d).wait()
-            for d in range(1, 4):
-                back_one(q, d).start()
-        yield
-        for q in range(3):
-            for d in range(1, 4):
-                back_one(q, d).wait()
-            back_pair(q).start()
-        yield
-        for q in range(3):
-            back_pair(q).wait()
+            back_pair(q, 0).start()
+        yield
+        for d in (1, 3, 2):
+            for q in range(3):
+                for k in range(4):
+                    back_one(q, d, k).wait()
+                back_pair(q, d).start()
+        yield
+        for d in (0, 1, 3, 2):
+            for q in range(3):
+                back_pair(q, d).wait()
         yield
 
     def gain_reduce():
@@ -496,69 +532,52 @@
         for i in range(4 * g, min(4 * g + 4, OWN)):
             data_copy(i).wait_recv()
         back_a(g)
+        if g < N_GROUP - 1:
+            back_b(g)
+            back_c(g)
     put(a1, 0, dot(mixed_t[...], ret[...].reshape(TOK, D)))
     put(a1, 4 * D, dot(norm_t[...], gh_all[:, 0:D]))
     a1[8 * D : ROWS1, :] = jnp.zeros((ROWS1 - 8 * D, 128), BF)
     next(red1)
-    back_b(0)
+    back_b(3)
     next(red1)
-    back_b(1)
-    back_b(2)
-    next(red1)
-    back_b(3)
     for k in range(3):
         put(a2, k * 4 * D, dot(norm_t[...], gh_all[:, (k + 1) * D : (k + 2) * D]))
     next(red2)
     next(red1)
-    back_c(0)
+    back_c(3)
     next(red2)
-    next(red1)
-    back_c(1)
-    next(red1)
-    back_c(2)
-    next(red2)
-    back_c(3)
-
-    owner = jnp.broadcast_to(owner_ref[...].astype(F32), (UNIQ, UNIQ))
-    owner_col = jnp.transpose(owner)
-    before = iota((UNIQ, UNIQ), 0) < iota((UNIQ, UNIQ), 1)
-    rank = jnp.sum(jnp.where((owner == owner_col) & before, 1.0, 0.0), axis=0, keepdims=True)
-    mine = iota((N_DEV, UNIQ), 0) == owner_ref[...]
-    lanes = iota((N_DEV, 128), 1)
+
     row_half = rows_acc[...].astype(BF)
-    ids_all = jnp.zeros((N_DEV, 128), F32)
-    order_f = orow_ref[...].astype(F32)
     for c in range(CAP):
-        sel = jnp.where(mine & (rank == float(c)), 1.0, 0.0)
-        ids = jnp.sum(sel * order_f, axis=1, keepdims=True)
-        ids_all = jnp.where(lanes == c, ids, ids_all)
-        picked = dot(sel.astype(BF), row_half)
+        picked = dot(sel_all[c], row_half)
         for k in range(4):
             spread[pl.ds(k * CAP + c, N_DEV, stride=16), :] = picked[:, k * 128 : (k + 1) * 128]
     send[...] = spread[...].astype(BF).reshape(N_DEV, 16, 128)
-    meta[...] = ids_all.reshape(N_DEV, 1, 128)
 
     next(red_g)
 
     def scatter_out(i, carry):
         other, to = device(i)
         remote(send.at[other], got_ref.at[i], asem, (0,), to).start()
-        remote(meta.at[other], gotm_ref.at[i], asem, (1,), to).start()
         return carry
 
     lax.fori_loop(1, N_DEV, scatter_out, 0)
     got_ref[0] = send[me]
-    gotm_ref[0] = meta[me]
-
-    next(red2)
-    next(red_g)
+
     next(red1)
-    next(red2)
     next(red_g)
     next(red2)
+    next(red1)
     next(red_g)
     next(red2)
+    next(red1)
     next(red_g)
+    next(red2)
+    next(red1)
+    next(red_g)
+    next(red2)
+    next(red2)
     next(red1)
     others = pl.ds(1, N_DEV - 1)
     remote(send.at[others], got_ref.at[others], asem, (0,), partner).wait()
@@ -607,6 +626,7 @@
         v((N_DEV * 16, 128), F32),
         v((N_DEV, 16, 128), BF),
         v((N_DEV, 1, 128), F32),
+        v((CAP, N_DEV, UNIQ), BF),
         v((ROWS1, 128), BF),
         v((ROWS2, 128), BF),
     ]
@@ -615,8 +635,9 @@
             scratch.append(v(shape[:-1] + (shape[-1] * ch, 128), BF))
     scratch += [
         v((4, 4, 8, 128), F32),
-        dma((2, 2, 2, 3)),
-        dma((2, 2, 5, 3, 3)),
+        dma((2, 2, 2, 3, 4)),
+        dma((2, 2, 4, 3, 3)),
+        dma((2, 2, 3, 3, 4)),
         dma((2, 2)),
         dma((2, 4, 3)),
     ]
@@ -724,7 +745,7 @@
             pltpu.VMEM((CAP * N_DEV, D), BF),
             pltpu.VMEM((128, N_DEV), F32),
         ],
-        compiler_params=pltpu.CompilerParams(vmem_limit_bytes=40 << 20),
+        compiler_params=pltpu.CompilerParams(vmem_limit_bytes=67_000_000),
         name="finish",
     )(g1, g1, g2, got.reshape(N_DEV * 16, 128), meta, gains)
 

time: 91.2 us -> 84.9 us (0.931)
  local copies, waits for them, and re-layouts: 5.23 us -> 0 us
    unnamed x10 -> x0, local copies, waits for them, and re-layouts: 5.23 us -> none
    pallas_call x1, Pallas kernels: 81 us -> 77.8 us  [run_step(): pl.pallas_call(step_kernel, out_shape=(jax.ShapeDtypeStruct((ROWS1, 128),...]
    pallas_call x1, Pallas kernels: 3.97 us -> 6.29 us  [finish(): pl.pallas_call(body, out_shape=(jax.ShapeDtypeStruct((ROWS_DEV, D), F32),...]
where the time goes in v1:
time: 84.9 us; the launch traced here: 84.7 us
  Pallas kernels  84.1 us (99%)
    pallas_call x1, Pallas kernels, run_step(): pl.pallas_call(step_kernel, out_shape=(jax.ShapeDtypeStruct((ROWS1, 128),...  77.8 us
    pallas_call x1, Pallas kernels, finish(): pl.pallas_call(body, out_shape=(jax.ShapeDtypeStruct((ROWS_DEV, D), F32),...  6.29 us

profile of v1, /device:TPU:1, one launch (start us, length us, event | category | flops | bytes accessed | tf_op | source)
XLA Modules:
  0.0 84.7 jit_solution(17835147435640922259)
XLA Ops:
  0.6 77.8 %step.1 = (bf16[4608,128]{1,0:T(8,128)(2,1)}, bf16[6144,128]{1,0:T(8,128)(2,1)}, bf16[128,16,128]{2,1,0:T(8,128)(2,1)}, f32[128,1,128]{2,1,0:T(1,128)}, f32[8,128]{1,0:T(8,128)}) custom-call(s32[16]{0:T(128)} %dest_s.1, s32[1,16]{1,0:T(1,128)} %bitcast.14, s32[1,16]{1,0:T(1,128)} %bitcast.17, s32[8,128]{1,0:T(8,128)} %bitcast.11, s32[1,256]{1,0:T(1,128)} %bitcast.15, ...), custom_call_target="tpu_custom_call" | custom-call | tf_op jit(solution)/shard_map/step/pallas_call | solution.py:644
  78.4 6.3 %finish.1 = (f32[1024,512]{1,0:T(8,128)}, f32[512,2048]{1,0:T(8,128)}, f32[512,512]{1,0:T(8,128)}, f32[1,512]{1,0:T(1,128)}, f32[1,512]{1,0:T(1,128)}) custom-call(bf16[4608,128]{1,0:T(8,128)(2,1)} %get-tuple-element.15.refs_0_.refs_1_, bf16[4608,128]{1,0:T(8,128)(2,1)} %get-tuple-element.15.refs_0_.refs_1_, bf16[6144,128]{1,0:T(8,128)(2,1)} %get-tuple-element.16.refs_2_, ...), custom_call_target="tpu_custom_call" | custom-call | tf_op jit(solution)/shard_map/finish/pallas_call | solution.py:718

commit v2 on v1

--- a/solution.py
+++ b/solution.py
@@ -80,11 +80,11 @@
     grad_hbm,
     w_in_hbm,
     w_out_hbm,
-    g1_ref,
-    g2_ref,
-    got_ref,
-    gotm_ref,
-    gains_ref,
+    g1_out,
+    g2_out,
+    picked_out,
+    ids_out,
+    gains_out,
     touched,
     grad_bal,
     w_in,
@@ -97,7 +97,8 @@
     ret,
     lsem,
     dsem,
-    own_sem,
+    ready,
+    out_sem,
     hot_all,
     norm_t,
     mixed_t,
@@ -138,6 +139,13 @@
     bsem,
     asem,
     gsem,
+    g1_ref,
+    g2_ref,
+    got_ref,
+    gotm_ref,
+    picked_ref,
+    ids_ref,
+    gains_ref,
 ):
     dp = lax.axis_index("dp")
     tb = lax.axis_index("table")
@@ -187,11 +195,13 @@
 
     barrier = pltpu.get_barrier_semaphore()
 
-    def greet(i, carry):
-        pl.semaphore_signal(barrier, inc=1, device_id=device(i)[1], device_id_type=MESH)
-        return carry
-
-    lax.fori_loop(1, N_DEV, greet, 0)
+    def column(i):
+        return (dp, lax.rem(tb + i, N_TABLE))
+
+    for i in range(OWN):
+        pl.semaphore_signal(barrier, inc=1, device_id=(plus(i), tb), device_id_type=MESH)
+    for i in range(1, N_TABLE):
+        pl.semaphore_signal(barrier, inc=1, device_id=column(i), device_id_type=MESH)
 
     hits = dest_l[...] == iota((N_DP, N_DP), 0)
     lengths = jnp.sum(
@@ -270,7 +280,7 @@
     loads[1].wait()
     forward(0)
 
-    pl.semaphore_wait(barrier, N_DEV - 1)
+    pl.semaphore_wait(barrier, OWN + N_TABLE - 1)
 
     def len_copy(i):
         return remote(lens.at[minus(i)], got_len.at[dp], lsem, (i,), (minus(i), tb))
@@ -278,6 +288,8 @@
     for i in range(OWN):
         len_copy(i).start()
     got_len[dp] = lens[dp]
+    for i in range(1, N_TABLE):
+        pl.semaphore_signal(ready, inc=1, device_id=column(i), device_id_type=MESH)
     owner = jnp.broadcast_to(owner_ref[...].astype(F32), (UNIQ, UNIQ))
     owner_col = jnp.transpose(owner)
     before = iota((UNIQ, UNIQ), 0) < iota((UNIQ, UNIQ), 1)
@@ -328,6 +340,7 @@
         remote(meta.at[other], gotm_ref.at[i], asem, (1,), to).start()
         return carry
 
+    pl.semaphore_wait(ready, N_TABLE - 1)
     lax.fori_loop(1, N_DEV, meta_out, 0)
     gotm_ref[0] = meta[me]
 
@@ -534,7 +547,6 @@
         back_a(g)
         if g < N_GROUP - 1:
             back_b(g)
-            back_c(g)
     put(a1, 0, dot(mixed_t[...], ret[...].reshape(TOK, D)))
     put(a1, 4 * D, dot(norm_t[...], gh_all[:, 0:D]))
     a1[8 * D : ROWS1, :] = jnp.zeros((ROWS1 - 8 * D, 128), BF)
@@ -545,8 +557,13 @@
         put(a2, k * 4 * D, dot(norm_t[...], gh_all[:, (k + 1) * D : (k + 2) * D]))
     next(red2)
     next(red1)
+    back_c(0)
+    next(red2)
+    back_c(1)
+    next(red1)
+    back_c(2)
     back_c(3)
-    next(red2)
+    next(red_g)
 
     row_half = rows_acc[...].astype(BF)
     for c in range(CAP):
@@ -554,37 +571,61 @@
         for k in range(4):
             spread[pl.ds(k * CAP + c, N_DEV, stride=16), :] = picked[:, k * 128 : (k + 1) * 128]
     send[...] = spread[...].astype(BF).reshape(N_DEV, 16, 128)
-
-    next(red_g)
+    got_ref[0] = send[me]
 
     def scatter_out(i, carry):
         other, to = device(i)
         remote(send.at[other], got_ref.at[i], asem, (0,), to).start()
         return carry
 
-    lax.fori_loop(1, N_DEV, scatter_out, 0)
-    got_ref[0] = send[me]
-
+    next(red2)
+    lax.fori_loop(1, 49, scatter_out, 0)
     next(red1)
     next(red_g)
+    lax.fori_loop(49, 81, scatter_out, 0)
+    next(red2)
+    next(red1)
+    next(red_g)
+    lax.fori_loop(81, N_DEV, scatter_out, 0)
     next(red2)
     next(red1)
     next(red_g)
     next(red2)
+    next(red_g)
     next(red1)
-    next(red_g)
-    next(red2)
-    next(red1)
-    next(red_g)
-    next(red2)
-    next(red2)
-    next(red1)
+
+    def out_copy(src, dst, n):
+        return pltpu.make_async_copy(src, dst, out_sem.at[n])
+
+    outs = [out_copy(g1_ref, g1_out, 0), out_copy(gains_ref, gains_out, 1)]
+    for o in outs:
+        o.start()
     others = pl.ds(1, N_DEV - 1)
     remote(send.at[others], got_ref.at[others], asem, (0,), partner).wait()
     remote(meta.at[others], gotm_ref.at[others], asem, (1,), partner).wait()
+    next(red2)
+    half = pl.ds(pl.multiple_of(core * (ROWS2 // 2), 16), ROWS2 // 2)
+    rest = pl.ds(pl.multiple_of((1 - core) * (ROWS2 // 2), 16), ROWS2 // 2)
+    outs.append(out_copy(g2_ref.at[half], g2_out.at[half], 2))
+    outs[-1].start()
+    spread[...] = got_ref[...].reshape(N_DEV * 16, 128).astype(F32)
+    for c in range(CAP):
+        for k in range(4):
+            picked_ref[c * N_DEV : (c + 1) * N_DEV, k * 128 : (k + 1) * 128] = spread[
+                pl.ds(k * CAP + c, N_DEV, stride=16), :
+            ].astype(BF)
+    ids_ref[...] = jnp.transpose(gotm_ref[...].reshape(N_DEV, 128))
+    outs.append(out_copy(picked_ref, picked_out, 3))
+    outs[-1].start()
+    outs.append(out_copy(ids_ref, ids_out, 4))
+    outs[-1].start()
     for i in range(OWN):
         data_copy(i).wait_send()
     next(red2)
+    outs.append(out_copy(g2_ref.at[rest], g2_out.at[rest], 5))
+    outs[-1].start()
+    for o in outs:
+        o.wait()
 
 
 def run_step(seq_dest, seq_blocks, items, owner, orow, gain_in, gain_out, touched, grad_out, w_in, w_out):
@@ -606,7 +647,8 @@
         v((N_DP, SLOT, D), BF),
         dma((2, N_DP)),
         dma((2, N_DP)),
-        dma((1,)),
+        pltpu.SemaphoreType.REGULAR,
+        dma((6,)),
         v((UNIQ, TOK), BF),
         v((D, TOK), BF),
         v((D, TOK), BF),
@@ -640,18 +682,25 @@
         dma((2, 2, 3, 3, 4)),
         dma((2, 2)),
         dma((2, 4, 3)),
+        v((ROWS1, 128), BF),
+        v((ROWS2, 128), BF),
+        v((N_DEV, 16, 128), BF),
+        v((N_DEV, 1, 128), F32),
+        v((CAP * N_DEV, D), BF),
+        v((128, N_DEV), F32),
+        v((8, 128), F32),
     ]
     return pl.pallas_call(
         step_kernel,
         out_shape=(
             jax.ShapeDtypeStruct((ROWS1, 128), BF),
             jax.ShapeDtypeStruct((ROWS2, 128), BF),
-            jax.ShapeDtypeStruct((N_DEV, 16, 128), BF),
-            jax.ShapeDtypeStruct((N_DEV, 1, 128), F32),
+            jax.ShapeDtypeStruct((CAP * N_DEV, D), BF),
+            jax.ShapeDtypeStruct((128, N_DEV), F32),
             jax.ShapeDtypeStruct((8, 128), F32),
         ),
         in_specs=[smem] + [vmem] * 7 + [far] * 4,
-        out_specs=(vmem,) * 5,
+        out_specs=(far,) * 5,
         scratch_shapes=scratch,
         compiler_params=pltpu.CompilerParams(
             collective_id=0, has_side_effects=True, vmem_limit_bytes=67_000_000
@@ -674,7 +723,7 @@
 
 
 def finish_kernel(
-    out_ref, gate_ref, rest_ref, got_ref, meta_ref, gains_in, table_ref, win_ref, wout_ref, gin_ref, gout_ref, spread, picked, ids, *, factor
+    out_ref, gate_ref, rest_ref, picked_ref, ids_ref, gains_in, table_ref, win_ref, wout_ref, gin_ref, gout_ref, *, factor
 ):
     i = pl.program_id(0)
 
@@ -684,31 +733,30 @@
 
     @pl.when(i == 0)
     def _():
-        spread[...] = got_ref[...].astype(F32)
-        for c in range(CAP):
-            for k in range(4):
-                picked[c * N_DEV : (c + 1) * N_DEV, k * 128 : (k + 1) * 128] = spread[
-                    pl.ds(k * CAP + c, N_DEV, stride=16), :
-                ].astype(BF)
-        ids[...] = jnp.transpose(meta_ref[...].reshape(N_DEV, 128))
         for j in range(4):
             gin_ref[:, j * 128 : (j + 1) * 128] = gains_in[j : j + 1, :] * factor
             gout_ref[:, j * 128 : (j + 1) * 128] = gains_in[4 + j : 5 + j, :] * factor
         unpack(out_ref, wout_ref)
+
+    @pl.when(i == 1)
+    def _():
         unpack(gate_ref, win_ref)
+
+    @pl.when(i > 1)
+    def _():
+        unpack(rest_ref, win_ref)
 
     @pl.when(i > 0)
     def _():
-        unpack(rest_ref, win_ref)
-
-    rows = (iota((256, N_DEV), 0) + i * 256).astype(F32)
-    hot = jnp.concatenate(
-        [jnp.where(rows == ids[c : c + 1, :], 1.0, 0.0).astype(BF) for c in range(CAP)], axis=1
-    )
-    table_ref[...] = dot(hot, picked[...])
-
-
-def finish(g1, g2, got, meta, gains, factor):
+        rows = (iota((256, N_DEV), 0) + (i - 1) * 256).astype(F32)
+        hot = jnp.concatenate(
+            [jnp.where(rows == ids_ref[c : c + 1, :], 1.0, 0.0).astype(BF) for c in range(CAP)],
+            axis=1,
+        )
+        table_ref[...] = dot(hot, picked_ref[...])
+
+
+def finish(g1, g2, picked, ids, gains, factor):
     def fixed(*shape):
         return pl.BlockSpec(shape, lambda i: (0,) * len(shape))
 
@@ -724,30 +772,25 @@
             jax.ShapeDtypeStruct((1, D), F32),
             jax.ShapeDtypeStruct((1, D), F32),
         ),
-        grid=(4,),
+        grid=(5,),
         in_specs=[
             pl.BlockSpec((4 * D, 128), lambda i: (0, 0)),
             pl.BlockSpec((4 * D, 128), lambda i: (1, 0)),
-            pl.BlockSpec((4 * D, 128), lambda i: (jnp.maximum(i - 1, 0), 0)),
-            fixed(N_DEV * 16, 128),
-            fixed(N_DEV, 1, 128),
+            pl.BlockSpec((4 * D, 128), lambda i: (jnp.maximum(i - 2, 0), 0)),
+            fixed(CAP * N_DEV, D),
+            pl.BlockSpec((8, N_DEV), lambda i: (0, 0)),
             fixed(8, 128),
         ],
         out_specs=(
-            pl.BlockSpec((256, D), lambda i: (i, 0)),
-            pl.BlockSpec((D, D), lambda i: (0, i)),
+            pl.BlockSpec((256, D), lambda i: (jnp.maximum(i - 1, 0), 0)),
+            pl.BlockSpec((D, D), lambda i: (0, jnp.maximum(i - 1, 0))),
             fixed(D, D),
             fixed(1, D),
             fixed(1, D),
         ),
-        scratch_shapes=[
-            pltpu.VMEM((N_DEV * 16, 128), F32),
-            pltpu.VMEM((CAP * N_DEV, D), BF),
-            pltpu.VMEM((128, N_DEV), F32),
-        ],
         compiler_params=pltpu.CompilerParams(vmem_limit_bytes=67_000_000),
         name="finish",
-    )(g1, g1, g2, got.reshape(N_DEV * 16, 128), meta, gains)
+    )(g1, g1, g2, picked, ids, gains)
 
 
 def on_device(
@@ -763,7 +806,7 @@
     gain_in,
     gain_out,
 ):
-    g1, g2, got, meta, gains = run_step(
+    g1, g2, picked, ids, gains = run_step(
         seq_dest,
         seq_blocks,
         row_of_token,
@@ -777,7 +820,7 @@
         w_out,
     )
     factor = 1.0 / math.sqrt(grad_out.shape[0] * N_DEV)
-    table, grad_in, grad_w_out, gin, gout = finish(g1, g2, got, meta, gains, factor)
+    table, grad_in, grad_w_out, gin, gout = finish(g1, g2, picked, ids, gains, factor)
     return (table, grad_in, grad_w_out, gin.reshape(-1), gout.reshape(-1))
 
 

time: 84.9 us -> 82.4 us (0.971)
  Pallas kernels: 84.1 us -> 81.4 us
    pallas_call x1, Pallas kernels: 77.8 us -> 74.9 us  [run_step(): pl.pallas_call(step_kernel, out_shape=(jax.ShapeDtypeStruct((ROWS1, 128),...]
where the time goes in v2:
time: 82.4 us; the launch traced here: 82.2 us
  Pallas kernels  81.4 us (99%)
    pallas_call x1, Pallas kernels, run_step(): pl.pallas_call(step_kernel, out_shape=(jax.ShapeDtypeStruct((ROWS1, 128),...  74.9 us
    pallas_call x1, Pallas kernels, finish(): pl.pallas_call(body, out_shape=(jax.ShapeDtypeStruct((ROWS_DEV, D), F32),...  6.48 us

profile of v2, /device:TPU:1, one launch (start us, length us, event | category | flops | bytes accessed | tf_op | source)
XLA Modules:
  0.0 82.2 jit_solution(16342879643860425673)
XLA Ops:
  0.6 74.9 %step.1 = (bf16[4608,128]{1,0:T(8,128)(2,1)}, bf16[6144,128]{1,0:T(8,128)(2,1)}, bf16[512,512]{1,0:T(8,128)(2,1)}, f32[128,128]{1,0:T(8,128)}, f32[8,128]{1,0:T(8,128)}) custom-call(s32[16]{0:T(128)} %dest_s.1, s32[1,16]{1,0:T(1,128)} %bitcast.12, s32[1,16]{1,0:T(1,128)} %bitcast.15, s32[8,128]{1,0:T(8,128)} %bitcast.9, s32[1,256]{1,0:T(1,128)} %bitcast.13, ...), custom_call_target="tpu_custom_call" | custom-call | tf_op jit(solution)/shard_map/step/pallas_call | solution.py:693
  75.5 6.5 %finish.1 = (f32[1024,512]{1,0:T(8,128)}, f32[512,2048]{1,0:T(8,128)}, f32[512,512]{1,0:T(8,128)}, f32[1,512]{1,0:T(1,128)}, f32[1,512]{1,0:T(1,128)}) custom-call(bf16[4608,128]{1,0:T(8,128)(2,1)} %get-tuple-element.15.refs_0_.refs_1_, bf16[4608,128]{1,0:T(8,128)(2,1)} %get-tuple-element.15.refs_0_.refs_1_, bf16[6144,128]{1,0:T(8,128)(2,1)} %get-tuple-element.16.refs_2_, ...), custom_call_target="tpu_custom_call" | custom-call | tf_op jit(solution)/shard_map/finish/pallas_call | solution.py:766

commit v3 on v2

--- a/solution.py
+++ b/solution.py
@@ -276,10 +276,6 @@
         hat_out_all[here, :] = hat
         mixed_t[:, here] = jnp.transpose(hat * gain_out * gate_all[here, :]).astype(BF)
 
-    loads[0].wait()
-    loads[1].wait()
-    forward(0)
-
     pl.semaphore_wait(barrier, OWN + N_TABLE - 1)
 
     def len_copy(i):
@@ -290,6 +286,42 @@
     got_len[dp] = lens[dp]
     for i in range(1, N_TABLE):
         pl.semaphore_signal(ready, inc=1, device_id=column(i), device_id_type=MESH)
+    loads[0].wait()
+    loads[1].wait()
+    forward(0)
+    for i in range(OWN):
+        len_copy(i).wait()
+    loads[2].wait()
+    loads[3].wait()
+
+    start = jnp.zeros((1, D), jnp.int32)
+    for p in range(N_DP):
+        wide[p] = start
+        start = start + got_len[p]
+    row_id = iota((SLOT, D), 0)
+    col_id = iota((SLOT, D), 1)
+
+    def pick(p):
+        hit = (col_id == wide[p] * BLK + row_id) & (row_id < got_len[p] * BLK)
+        return hit.astype(F32).astype(BF)
+
+    def data_copy(i):
+        return remote(stage.at[i], ret.at[i], dsem, (i,), (minus(i), tb))
+
+    for g in range(N_GROUP):
+        hot = jnp.concatenate([pick(minus(4 * g + k)) for k in range(4)], axis=0)
+        slabs = dot(hot, grad_bal[...]).astype(BF)
+        for k in range(4):
+            i = 4 * g + k
+            slab = slabs[k * SLOT : (k + 1) * SLOT, :]
+            if i == OWN:
+                ret[OWN] = slab
+            else:
+                stage[i] = slab
+                data_copy(i).start()
+
+    forward(1)
+
     owner = jnp.broadcast_to(owner_ref[...].astype(F32), (UNIQ, UNIQ))
     owner_col = jnp.transpose(owner)
     before = iota((UNIQ, UNIQ), 0) < iota((UNIQ, UNIQ), 1)
@@ -303,37 +335,6 @@
         sel_all[c] = sel.astype(BF)
         ids_all = jnp.where(lanes == c, jnp.sum(sel * order_f, axis=1, keepdims=True), ids_all)
     meta[...] = ids_all.reshape(N_DEV, 1, 128)
-    forward(1)
-    for i in range(OWN):
-        len_copy(i).wait()
-    loads[2].wait()
-    loads[3].wait()
-
-    start = jnp.zeros((1, D), jnp.int32)
-    for p in range(N_DP):
-        wide[p] = start
-        start = start + got_len[p]
-    row_id = iota((SLOT, D), 0)
-    col_id = iota((SLOT, D), 1)
-
-    def pick(p):
-        hit = (col_id == wide[p] * BLK + row_id) & (row_id < got_len[p] * BLK)
-        return hit.astype(F32).astype(BF)
-
-    def data_copy(i):
-        return remote(stage.at[i], ret.at[i], dsem, (i,), (minus(i), tb))
-
-    for g in range(N_GROUP):
-        hot = jnp.concatenate([pick(minus(4 * g + k)) for k in range(4)], axis=0)
-        slabs = dot(hot, grad_bal[...]).astype(BF)
-        for k in range(4):
-            i = 4 * g + k
-            slab = slabs[k * SLOT : (k + 1) * SLOT, :]
-            if i == OWN:
-                ret[OWN] = slab
-            else:
-                stage[i] = slab
-                data_copy(i).start()
 
     def meta_out(i, carry):
         other, to = device(i)
@@ -723,42 +724,77 @@
 
 
 def finish_kernel(
-    out_ref, gate_ref, rest_ref, picked_ref, ids_ref, gains_in, table_ref, win_ref, wout_ref, gin_ref, gout_ref, *, factor
+    g1_hbm,
+    g2_hbm,
+    picked_hbm,
+    ids_ref,
+    gains_in,
+    table_out,
+    win_out,
+    wout_out,
+    gin_ref,
+    gout_ref,
+    g1,
+    g2,
+    picked,
+    table,
+    win,
+    wout,
+    in_sem,
+    out_sem,
+    *,
+    factor
 ):
-    i = pl.program_id(0)
-
-    def unpack(src, dst):
-        for j in range(4):
-            dst[:, j * 128 : (j + 1) * 128] = src[j * D : (j + 1) * D, :].astype(F32) * factor
-
-    @pl.when(i == 0)
-    def _():
-        for j in range(4):
-            gin_ref[:, j * 128 : (j + 1) * 128] = gains_in[j : j + 1, :] * factor
-            gout_ref[:, j * 128 : (j + 1) * 128] = gains_in[4 + j : 5 + j, :] * factor
-        unpack(out_ref, wout_ref)
-
-    @pl.when(i == 1)
-    def _():
-        unpack(gate_ref, win_ref)
-
-    @pl.when(i > 1)
-    def _():
-        unpack(rest_ref, win_ref)
-
-    @pl.when(i > 0)
-    def _():
-        rows = (iota((256, N_DEV), 0) + (i - 1) * 256).astype(F32)
+    part = 4 * D
+
+    def take(n):
+        if n == 0:
+            return pltpu.make_async_copy(picked_hbm, picked, in_sem.at[0])
+        far, near = (g1_hbm, g1) if n < 3 else (g2_hbm, g2)
+        rows = pl.ds(((n - 1) if n < 3 else (n - 3)) * part, part)
+        return pltpu.make_async_copy(far.at[rows], near.at[rows], in_sem.at[n])
+
+    def give(n):
+        if n < 4:
+            rows = pl.ds(n * 256, 256)
+            return pltpu.make_async_copy(table.at[rows], table_out.at[rows], out_sem.at[n])
+        if n == 4:
+            return pltpu.make_async_copy(wout, wout_out, out_sem.at[n])
+        cols = pl.ds((n - 5) * D, D)
+        return pltpu.make_async_copy(win.at[n - 5], win_out.at[:, cols], out_sem.at[n])
+
+    for n in range(6):
+        take(n).start()
+    for j in range(4):
+        gin_ref[:, j * 128 : (j + 1) * 128] = gains_in[j : j + 1, :] * factor
+        gout_ref[:, j * 128 : (j + 1) * 128] = gains_in[4 + j : 5 + j, :] * factor
+    take(0).wait()
+    for n in range(4):
+        rows = (iota((256, N_DEV), 0) + n * 256).astype(F32)
         hot = jnp.concatenate(
             [jnp.where(rows == ids_ref[c : c + 1, :], 1.0, 0.0).astype(BF) for c in range(CAP)],
             axis=1,
         )
-        table_ref[...] = dot(hot, picked_ref[...])
+        table[n * 256 : (n + 1) * 256, :] = dot(hot, picked[...])
+        give(n).start()
+    for n in range(5):
+        take(n + 1).wait()
+        src, first = (g1, n * part) if n < 2 else (g2, (n - 2) * part)
+        for j in range(4):
+            block = src[first + j * D : first + (j + 1) * D, :].astype(F32) * factor
+            cols = slice(j * 128, (j + 1) * 128)
+            if n == 0:
+                wout[:, cols] = block
+            else:
+                win[n - 1, :, cols] = block
+        give(4 + n).start()
+    for n in range(9):
+        give(n).wait()
 
 
 def finish(g1, g2, picked, ids, gains, factor):
-    def fixed(*shape):
-        return pl.BlockSpec(shape, lambda i: (0,) * len(shape))
+    far = pl.BlockSpec(memory_space=pl.ANY)
+    vmem = pl.BlockSpec(memory_space=pltpu.VMEM)
 
     def body(*refs):
         finish_kernel(*refs, factor=factor)
@@ -772,25 +808,21 @@
             jax.ShapeDtypeStruct((1, D), F32),
             jax.ShapeDtypeStruct((1, D), F32),
         ),
-        grid=(5,),
-        in_specs=[
-            pl.BlockSpec((4 * D, 128), lambda i: (0, 0)),
-            pl.BlockSpec((4 * D, 128), lambda i: (1, 0)),
-            pl.BlockSpec((4 * D, 128), lambda i: (jnp.maximum(i - 2, 0), 0)),
-            fixed(CAP * N_DEV, D),
-            pl.BlockSpec((8, N_DEV), lambda i: (0, 0)),
-            fixed(8, 128),
+        in_specs=[far] * 3 + [vmem] * 2,
+        out_specs=(far, far, far, vmem, vmem),
+        scratch_shapes=[
+            pltpu.VMEM((ROWS1, 128), BF),
+            pltpu.VMEM((ROWS2, 128), BF),
+            pltpu.VMEM((CAP * N_DEV, D), BF),
+            pltpu.VMEM((ROWS_DEV, D), F32),
+            pltpu.VMEM((4, D, D), F32),
+            pltpu.VMEM((D, D), F32),
+            pltpu.SemaphoreType.DMA((6,)),
+            pltpu.SemaphoreType.DMA((9,)),
         ],
-        out_specs=(
-            pl.BlockSpec((256, D), lambda i: (jnp.maximum(i - 1, 0), 0)),
-            pl.BlockSpec((D, D), lambda i: (0, jnp.maximum(i - 1, 0))),
-            fixed(D, D),
-            fixed(1, D),
-            fixed(1, D),
-        ),
         compiler_params=pltpu.CompilerParams(vmem_limit_bytes=67_000_000),
         name="finish",
-    )(g1, g1, g2, picked, ids, gains)
+    )(g1, g2, picked, ids, gains)
 
 
 def on_device(

time: 82.4 us -> 81.6 us (level)
  no operation moved by 1% of the time
where the time goes in v3:
time: 81.6 us; the launch traced here: 81.4 us
  Pallas kernels  80.6 us (99%)
  between operations  0.82 us (1%)
    pallas_call x1, Pallas kernels, run_step(): pl.pallas_call(step_kernel, out_shape=(jax.ShapeDtypeStruct((ROWS1, 128),...  74.7 us
    pallas_call x1, Pallas kernels, finish(): pl.pallas_call(body, out_shape=(jax.ShapeDtypeStruct((ROWS_DEV, D), F32),...  5.88 us

profile of v3, /device:TPU:1, one launch (start us, length us, event | category | flops | bytes accessed | tf_op | source)
XLA Modules:
  0.0 81.4 jit_solution(5094554971118112490)
XLA Ops:
  0.6 74.7 %step.1 = (bf16[4608,128]{1,0:T(8,128)(2,1)}, bf16[6144,128]{1,0:T(8,128)(2,1)}, bf16[512,512]{1,0:T(8,128)(2,1)}, f32[128,128]{1,0:T(8,128)}, f32[8,128]{1,0:T(8,128)}) custom-call(s32[16]{0:T(128)} %dest_s.1, s32[1,16]{1,0:T(1,128)} %bitcast.12, s32[1,16]{1,0:T(1,128)} %bitcast.15, s32[8,128]{1,0:T(8,128)} %bitcast.9, s32[1,256]{1,0:T(1,128)} %bitcast.13, ...), custom_call_target="tpu_custom_call" | custom-call | tf_op jit(solution)/shard_map/step/pallas_call | solution.py:694
  75.4 5.9 %finish.1 = (f32[1024,512]{1,0:T(8,128)}, f32[512,2048]{1,0:T(8,128)}, f32[512,512]{1,0:T(8,128)}, f32[1,512]{1,0:T(1,128)}, f32[1,512]{1,0:T(1,128)}) custom-call(bf16[4608,128]{1,0:T(8,128)(2,1)} %get-tuple-element.15.refs_0_, bf16[6144,128]{1,0:T(8,128)(2,1)} %get-tuple-element.16.refs_1_, bf16[512,512]{1,0:T(8,128)(2,1)} %get-tuple-element.17.refs_2_, ...), custom_call_target="tpu_custom_call" | custom-call | tf_op jit(solution)/shard_map/finish/pallas_call | solution.py:802

commit v4 on v3

--- a/solution.py
+++ b/solution.py
@@ -45,12 +45,7 @@
     return lax.dot_general(a, b, (((0,), (0,)), ((), ())), preferred_element_type=F32)
 
 
-OFFSETS = (
-    (0, 1), (1, 0), (3, 0), (0, 3),
-    (1, 1), (3, 3), (0, 2), (2, 0),
-    (1, 3), (3, 1), (1, 2), (2, 1),
-    (3, 2), (2, 3), (2, 2), (0, 0),
-)
+OFFSETS = tuple((i // 4, i % 4) for i in range(1, 16)) + ((0, 0),)
 OWN = 15
 ORDERS = (("x", "y", "z"), ("y", "z", "x"), ("z", "x", "y"))
 
@@ -80,11 +75,11 @@
     grad_hbm,
     w_in_hbm,
     w_out_hbm,
-    g1_out,
-    g2_out,
-    picked_out,
-    ids_out,
-    gains_out,
+    g1_ref,
+    g2_ref,
+    picked_ref,
+    ids_ref,
+    gains_ref,
     touched,
     grad_bal,
     w_in,
@@ -98,7 +93,6 @@
     lsem,
     dsem,
     ready,
-    out_sem,
     hot_all,
     norm_t,
     mixed_t,
@@ -139,13 +133,8 @@
     bsem,
     asem,
     gsem,
-    g1_ref,
-    g2_ref,
     got_ref,
     gotm_ref,
-    picked_ref,
-    ids_ref,
-    gains_ref,
 ):
     dp = lax.axis_index("dp")
     tb = lax.axis_index("table")
@@ -595,20 +584,10 @@
     next(red_g)
     next(red1)
 
-    def out_copy(src, dst, n):
-        return pltpu.make_async_copy(src, dst, out_sem.at[n])
-
-    outs = [out_copy(g1_ref, g1_out, 0), out_copy(gains_ref, gains_out, 1)]
-    for o in outs:
-        o.start()
     others = pl.ds(1, N_DEV - 1)
     remote(send.at[others], got_ref.at[others], asem, (0,), partner).wait()
     remote(meta.at[others], gotm_ref.at[others], asem, (1,), partner).wait()
     next(red2)
-    half = pl.ds(pl.multiple_of(core * (ROWS2 // 2), 16), ROWS2 // 2)
-    rest = pl.ds(pl.multiple_of((1 - core) * (ROWS2 // 2), 16), ROWS2 // 2)
-    outs.append(out_copy(g2_ref.at[half], g2_out.at[half], 2))
-    outs[-1].start()
     spread[...] = got_ref[...].reshape(N_DEV * 16, 128).astype(F32)
     for c in range(CAP):
         for k in range(4):
@@ -616,17 +595,9 @@
                 pl.ds(k * CAP + c, N_DEV, stride=16), :
             ].astype(BF)
     ids_ref[...] = jnp.transpose(gotm_ref[...].reshape(N_DEV, 128))
-    outs.append(out_copy(picked_ref, picked_out, 3))
-    outs[-1].start()
-    outs.append(out_copy(ids_ref, ids_out, 4))
-    outs[-1].start()
     for i in range(OWN):
         data_copy(i).wait_send()
     next(red2)
-    outs.append(out_copy(g2_ref.at[rest], g2_out.at[rest], 5))
-    outs[-1].start()
-    for o in outs:
-        o.wait()
 
 
 def run_step(seq_dest, seq_blocks, items, owner, orow, gain_in, gain_out, touched, grad_out, w_in, w_out):
@@ -649,7 +620,6 @@
         dma((2, N_DP)),
         dma((2, N_DP)),
         pltpu.SemaphoreType.REGULAR,
-        dma((6,)),
         v((UNIQ, TOK), BF),
         v((D, TOK), BF),
         v((D, TOK), BF),
@@ -683,28 +653,23 @@
         dma((2, 2, 3, 3, 4)),
         dma((2, 2)),
         dma((2, 4, 3)),
-        v((ROWS1, 128), BF),
-        v((ROWS2, 128), BF),
         v((N_DEV, 16, 128), BF),
         v((N_DEV, 1, 128), F32),
-        v((CAP * N_DEV, D), BF),
-        v((128, N_DEV), F32),
-        v((8, 128), F32),
     ]
     return pl.pallas_call(
         step_kernel,
         out_shape=(
-            jax.ShapeDtypeStruct((ROWS1, 128), BF),
-            jax.ShapeDtypeStruct((ROWS2, 128), BF),
-            jax.ShapeDtypeStruct((CAP * N_DEV, D), BF),
-            jax.ShapeDtypeStruct((128, N_DEV), F32),
-            jax.ShapeDtypeStruct((8, 128), F32),
+            pltpu.VMEM((ROWS1, 128), BF),
+            pltpu.VMEM((ROWS2, 128), BF),
+            pltpu.VMEM((CAP * N_DEV, D), BF),
+            pltpu.VMEM((128, N_DEV), F32),
+            pltpu.VMEM((8, 128), F32),
         ),
         in_specs=[smem] + [vmem] * 7 + [far] * 4,
-        out_specs=(far,) * 5,
+        out_specs=(vmem,) * 5,
         scratch_shapes=scratch,
         compiler_params=pltpu.CompilerParams(
-            collective_id=0, has_side_effects=True, vmem_limit_bytes=67_000_000
+            collective_id=0, has_side_effects=True, vmem_limit_bytes=60_000_000
         ),
         name="step",
     )(
@@ -724,9 +689,9 @@
 
 
 def finish_kernel(
-    g1_hbm,
-    g2_hbm,
-    picked_hbm,
+    g1,
+    g2,
+    picked,
     ids_ref,
     gains_in,
     table_out,
@@ -734,25 +699,14 @@
     wout_out,
     gin_ref,
     gout_ref,
-    g1,
-    g2,
-    picked,
     table,
     win,
     wout,
-    in_sem,
     out_sem,
     *,
     factor
 ):
     part = 4 * D
-
-    def take(n):
-        if n == 0:
-            return pltpu.make_async_copy(picked_hbm, picked, in_sem.at[0])
-        far, near = (g1_hbm, g1) if n < 3 else (g2_hbm, g2)
-        rows = pl.ds(((n - 1) if n < 3 else (n - 3)) * part, part)
-        return pltpu.make_async_copy(far.at[rows], near.at[rows], in_sem.at[n])
 
     def give(n):
         if n < 4:
@@ -763,12 +717,9 @@
         cols = pl.ds((n - 5) * D, D)
         return pltpu.make_async_copy(win.at[n - 5], win_out.at[:, cols], out_sem.at[n])
 
-    for n in range(6):
-        take(n).start()
     for j in range(4):
         gin_ref[:, j * 128 : (j + 1) * 128] = gains_in[j : j + 1, :] * factor
         gout_ref[:, j * 128 : (j + 1) * 128] = gains_in[4 + j : 5 + j, :] * factor
-    take(0).wait()
     for n in range(4):
         rows = (iota((256, N_DEV), 0) + n * 256).astype(F32)
         hot = jnp.concatenate(
@@ -778,7 +729,6 @@
         table[n * 256 : (n + 1) * 256, :] = dot(hot, picked[...])
         give(n).start()
     for n in range(5):
-        take(n + 1).wait()
         src, first = (g1, n * part) if n < 2 else (g2, (n - 2) * part)
         for j in range(4):
             block = src[first + j * D : first + (j + 1) * D, :].astype(F32) * factor
@@ -808,19 +758,15 @@
             jax.ShapeDtypeStruct((1, D), F32),
             jax.ShapeDtypeStruct((1, D), F32),
         ),
-        in_specs=[far] * 3 + [vmem] * 2,
+        in_specs=[vmem] * 5,
         out_specs=(far, far, far, vmem, vmem),
         scratch_shapes=[
-            pltpu.VMEM((ROWS1, 128), BF),
-            pltpu.VMEM((ROWS2, 128), BF),
-            pltpu.VMEM((CAP * N_DEV, D), BF),
             pltpu.VMEM((ROWS_DEV, D), F32),
             pltpu.VMEM((4, D, D), F32),
             pltpu.VMEM((D, D), F32),
-            pltpu.SemaphoreType.DMA((6,)),
             pltpu.SemaphoreType.DMA((9,)),
         ],
-        compiler_params=pltpu.CompilerParams(vmem_limit_bytes=67_000_000),
+        compiler_params=pltpu.CompilerParams(vmem_limit_bytes=24_000_000),
         name="finish",
     )(g1, g2, picked, ids, gains)
 

time: 81.6 us -> 78.5 us (0.962)
  Pallas kernels: 80.6 us -> 77.6 us
    pallas_call x1, Pallas kernels: 5.88 us -> 3.94 us  [finish(): pl.pallas_call(body, out_shape=(jax.ShapeDtypeStruct((ROWS_DEV, D), F32),...]
    pallas_call x1, Pallas kernels: 74.7 us -> 73.6 us  [run_step(): pl.pallas_call(step_kernel, out_shape=(pltpu.VMEM((ROWS1, 128), BF), pltp...]
where the time goes in v4:
time: 78.5 us; the launch traced here: 78.4 us
  Pallas kernels  77.6 us (99%)
  between operations  0.82 us (1%)
    pallas_call x1, Pallas kernels, run_step(): pl.pallas_call(step_kernel, out_shape=(pltpu.VMEM((ROWS1, 128), BF), pltp...  73.6 us
    pallas_call x1, Pallas kernels, finish(): pl.pallas_call(body, out_shape=(jax.ShapeDtypeStruct((ROWS_DEV, D), F32),...  3.94 us

profile of v4, /device:TPU:1, one launch (start us, length us, event | category | flops | bytes accessed | tf_op | source)
XLA Modules:
  0.0 78.4 jit_solution(5823766737420507712)
XLA Ops:
  0.6 73.6 %step.1 = (bf16[4608,128]{1,0:T(8,128)(2,1)S(1)}, bf16[6144,128]{1,0:T(8,128)(2,1)S(1)}, bf16[512,512]{1,0:T(8,128)(2,1)S(1)}, f32[128,128]{1,0:T(8,128)S(1)}, f32[8,128]{1,0:T(8,128)S(1)}) custom-call(s32[16]{0:T(128)} %dest_s.1, s32[1,16]{1,0:T(1,128)} %bitcast.12, s32[1,16]{1,0:T(1,128)} %bitcast.15, s32[8,128]{1,0:T(8,128)} %bitcast.9, ...), custom_call_target="tpu_custom_call" | custom-call | tf_op jit(solution)/shard_map/step/pallas_call | solution.py:659
  74.3 3.9 %finish.1 = (f32[1024,512]{1,0:T(8,128)}, f32[512,2048]{1,0:T(8,128)}, f32[512,512]{1,0:T(8,128)}, f32[1,512]{1,0:T(1,128)}, f32[1,512]{1,0:T(1,128)}) custom-call(bf16[4608,128]{1,0:T(8,128)(2,1)S(1)} %get-tuple-element.15.refs_0_, bf16[6144,128]{1,0:T(8,128)(2,1)S(1)} %get-tuple-element.16.refs_1_, bf16[512,512]{1,0:T(8,128)(2,1)S(1)} %get-tuple-element.17.refs_2_, ...), custom_call_target="tpu_custom_call" | custom-call | tf_op jit(solution)/shard_map/finish/pallas_call | solution.py:752

commit v5 on v4

--- a/solution.py
+++ b/solution.py
@@ -535,14 +535,15 @@
         for i in range(4 * g, min(4 * g + 4, OWN)):
             data_copy(i).wait_recv()
         back_a(g)
-        if g < N_GROUP - 1:
+        if g < N_GROUP - 2:
             back_b(g)
     put(a1, 0, dot(mixed_t[...], ret[...].reshape(TOK, D)))
     put(a1, 4 * D, dot(norm_t[...], gh_all[:, 0:D]))
     a1[8 * D : ROWS1, :] = jnp.zeros((ROWS1 - 8 * D, 128), BF)
     next(red1)
+    back_b(2)
+    next(red1)
     back_b(3)
-    next(red1)
     for k in range(3):
         put(a2, k * 4 * D, dot(norm_t[...], gh_all[:, (k + 1) * D : (k + 2) * D]))
     next(red2)
@@ -582,12 +583,12 @@
     next(red_g)
     next(red2)
     next(red_g)
+    next(red2)
     next(red1)
 
     others = pl.ds(1, N_DEV - 1)
     remote(send.at[others], got_ref.at[others], asem, (0,), partner).wait()
     remote(meta.at[others], gotm_ref.at[others], asem, (1,), partner).wait()
-    next(red2)
     spread[...] = got_ref[...].reshape(N_DEV * 16, 128).astype(F32)
     for c in range(CAP):
         for k in range(4):

time: 78.5 us -> 77.2 us (0.983)
  Pallas kernels: 77.6 us -> 76.2 us
    pallas_call x1, Pallas kernels: 73.6 us -> 72.3 us  [run_step(): pl.pallas_call(step_kernel, out_shape=(pltpu.VMEM((ROWS1, 128), BF), pltp...]
where the time goes in v5:
time: 77.2 us; the launch traced here: 77 us
  Pallas kernels  76.2 us (99%)
  between operations  0.82 us (1%)
    pallas_call x1, Pallas kernels, run_step(): pl.pallas_call(step_kernel, out_shape=(pltpu.VMEM((ROWS1, 128), BF), pltp...  72.3 us
    pallas_call x1, Pallas kernels, finish(): pl.pallas_call(body, out_shape=(jax.ShapeDtypeStruct((ROWS_DEV, D), F32),...  3.94 us

profile of v5, /device:TPU:1, one launch (start us, length us, event | category | flops | bytes accessed | tf_op | source)
XLA Modules:
  0.0 77.0 jit_solution(14919876128456924250)
XLA Ops:
  0.6 72.3 %step.1 = (bf16[4608,128]{1,0:T(8,128)(2,1)S(1)}, bf16[6144,128]{1,0:T(8,128)(2,1)S(1)}, bf16[512,512]{1,0:T(8,128)(2,1)S(1)}, f32[128,128]{1,0:T(8,128)S(1)}, f32[8,128]{1,0:T(8,128)S(1)}) custom-call(s32[16]{0:T(128)} %dest_s.1, s32[1,16]{1,0:T(1,128)} %bitcast.12, s32[1,16]{1,0:T(1,128)} %bitcast.15, s32[8,128]{1,0:T(8,128)} %bitcast.9, ...), custom_call_target="tpu_custom_call" | custom-call | tf_op jit(solution)/shard_map/step/pallas_call | solution.py:660
  72.9 3.9 %finish.1 = (f32[1024,512]{1,0:T(8,128)}, f32[512,2048]{1,0:T(8,128)}, f32[512,512]{1,0:T(8,128)}, f32[1,512]{1,0:T(1,128)}, f32[1,512]{1,0:T(1,128)}) custom-call(bf16[4608,128]{1,0:T(8,128)(2,1)S(1)} %get-tuple-element.15.refs_0_, bf16[6144,128]{1,0:T(8,128)(2,1)S(1)} %get-tuple-element.16.refs_1_, bf16[512,512]{1,0:T(8,128)(2,1)S(1)} %get-tuple-element.17.refs_2_, ...), custom_call_target="tpu_custom_call" | custom-call | tf_op jit(solution)/shard_map/finish/pallas_call | solution.py:753
